TPU v7x, 32 devices: a whole 2x2x4 slice. The times are simulated.
32 devices in a mesh: gx: 16 (over z, y, x), gy: 2 (over core).
Axes of the slice: x: 2, y: 2, z: 4, core: 2. Of those that a mesh axis runs over, the one named last changes fastest.
Arguments:
- density: float32 [128, 32, 64], P('gx', None, 'gy'), may hold values from 0.5 to 1.5
- momentum: float32 [3, 128, 32, 64], P(None, 'gx', None, 'gy'), may hold values from -3 to 3
- energy: float32 [128, 32, 64], P('gx', None, 'gy'), may hold values from 2.5 to 4
- eddy_normal_cell: int32 [1024], P('gx'), may hold values from 0 to 63
- eddy_spanwise_cell: int32 [1024], P('gx'), may hold values from 0 to 31
- eddy_signs: int32 [1024, 3], P('gx'), may hold values from 0 to 1
- eddy_strengths: float32 [1024], P('gx'), may hold values from 0.3 to 3
- filter_matrices: float32 [1, 128, 128], replicated, may hold values from -1.25 to 1.25
- shock_switch: int32 [1, 64], P(None, 'gy'), may hold values 0 or 1
- dilatation_bin: int32 [128, 32, 64], P('gx', None, 'gy'), may hold values from 0 to 63
- vorticity_bin: int32 [128, 32, 64], P('gx', None, 'gy'), may hold values from 0 to 63, as said below
Outputs:
- conserved_next: float32 [5, 128, 32, 64], P(None, 'gx', None, 'gy')
- histogram: float32 [64, 64], replicated
Inputs may be any that keep to these rules, and one draw needn't show every extreme that they name: vorticity_bin at streamwise cell x is x * 64 // 128 or one more, modulo 64.
All inputs are finite; a program needn't handle non-finite values. No bound on the sum of `shock_switch` on one device may be relied on, other than what follows from the above.
Results may differ from a plain program's by a relative error of at most 0.0003.
Values sent between devices are 32-bit elements; how exact they have to be, the bound alone decides.
No kernel may reach another device: no remote copies, remote signals or barrier semaphores. Data moves between devices by JAX's collectives and lax.ppermute only.
A program may use at most 64 MiB of HBM per device.

v0:
```python
import math
import jax
import jax.numpy as jnp
from jax import lax
from jax.sharding import PartitionSpec as P

HISTOGRAM_BINS = 64
SIGMA_Y = 32
SIGMA_Z = 8
TIME_STEP = 0.1
GAMMA_GAS = 1.4
SENSOR_EPS = 0.1
HAT_PEAK = math.sqrt(1.5)


def extended(x, sides, width):
    for axis, dim in sides:
        size, length = (lax.axis_size(axis), x.shape[dim])
        up = [(i, (i + 1) % size) for i in range(size - 1)]
        down = [(j, i) for i, j in up]
        last = lax.slice_in_dim(x, length - width, length, axis=dim)
        first = lax.slice_in_dim(x, 0, width, axis=dim)
        before = lax.ppermute(last, axis, up)
        after = lax.ppermute(first, axis, down)
        x = jnp.concatenate([before, x, after], axis=dim)
    return x


def hat_shape(centres, coords, spread, period):
    offset = coords[None, :] - centres[:, None]
    if period > 0:
        offset = jnp.mod(offset + period / 2, period) - period / 2
    return HAT_PEAK * jnp.maximum(0.0, 1.0 - jnp.abs(offset) / spread)


def inflow_from(centre_y, centre_z, eddy_weight, coords_y, coords_z, span):
    shape_y = hat_shape(centre_y, coords_y, float(SIGMA_Y), 0)
    shape_z = hat_shape(centre_z, coords_z, float(SIGMA_Z), span)
    weighted = (eddy_weight[:, :, None] * shape_z[:, None, :]).reshape(eddy_weight.shape[0], -1)
    inflow = jnp.dot(weighted.T, shape_y, precision=lax.Precision.HIGHEST)
    return inflow.reshape(3, coords_z.shape[0], coords_y.shape[0])


def ghost_state(inflow):
    mom_x = 1.0 + inflow[0]
    kinetic = mom_x * mom_x + inflow[1] * inflow[1] + inflow[2] * inflow[2]
    return jnp.stack([jnp.ones_like(mom_x), mom_x, inflow[1], inflow[2], 3.0 + 0.5 * kinetic])


def flux_of(fields, velocity, pressure, direction):
    result = fields * velocity[direction][None]
    result = result.at[1 + direction].add(pressure)
    return result.at[4].add(pressure * velocity[direction])


def central_x(values):
    return (values[..., 2:, :, 1:-1] - values[..., :-2, :, 1:-1]) * 0.5


def central_y(values):
    return (values[..., 1:-1, :, 2:] - values[..., 1:-1, :, :-2]) * 0.5


def central_z(values):
    centre = values[..., 1:-1, :, 1:-1]
    return (jnp.roll(centre, -1, axis=-2) - jnp.roll(centre, 1, axis=-2)) * 0.5


def section_rhs(padded):
    velocity = padded[1:4] / padded[0][None]
    pressure = (GAMMA_GAS - 1.0) * (padded[4] - 0.5 * jnp.sum(padded[1:4] * velocity, axis=0))
    change = central_x(flux_of(padded, velocity, pressure, 0))
    change = change + central_y(flux_of(padded, velocity, pressure, 1))
    change = change + central_z(flux_of(padded, velocity, pressure, 2))
    updated = padded[:, 1:-1, :, 1:-1] - TIME_STEP * change
    dilatation = central_x(velocity[0]) + central_y(velocity[1]) + central_z(velocity[2])
    vort_x = central_y(velocity[2]) - central_z(velocity[1])
    vort_y = central_z(velocity[0]) - central_x(velocity[2])
    vort_z = central_x(velocity[1]) - central_y(velocity[0])
    squared = dilatation * dilatation
    shock_sensor = squared / (
        squared + vort_x * vort_x + vort_y * vort_y + vort_z * vort_z + SENSOR_EPS
    )
    return (updated, shock_sensor)


def filter_lines(pencil, filter_matrices):
    block_count, block_len = (filter_matrices.shape[0], filter_matrices.shape[1])
    lanes = pencil.shape[2]
    blocks = pencil.reshape(5, block_count, block_len, lanes)
    smooth = jnp.einsum("bij,fbjp->fbip", filter_matrices, blocks, precision=lax.Precision.HIGHEST)
    return smooth.reshape(5, block_count * block_len, lanes)


def plane_histogram(shock_sensor, dilatation_bin, vorticity_bin):
    bin_levels = jnp.arange(HISTOGRAM_BINS, dtype=jnp.int32)

    def accumulate_plane(histogram_totals, histogram_parts):
        sensor_plane, plane_dilatation, plane_vorticity = histogram_parts
        flat_sensor = sensor_plane.reshape(-1)
        dilatation_table = (plane_dilatation.reshape(-1)[None, :] == bin_levels[:, None]).astype(
            jnp.float32
        )
        vorticity_table = jnp.where(
            plane_vorticity.reshape(-1)[:, None] == bin_levels[None, :], flat_sensor[:, None], 0.0
        )
        return (
            histogram_totals
            + jnp.dot(dilatation_table, vorticity_table, precision=lax.Precision.HIGHEST),
            None,
        )

    histogram_totals, _ = lax.scan(
        accumulate_plane,
        jnp.zeros((HISTOGRAM_BINS, HISTOGRAM_BINS), jnp.float32),
        (shock_sensor, dilatation_bin, vorticity_bin),
    )
    return histogram_totals


def shards(
    density,
    momentum,
    energy,
    eddy_normal_cell,
    eddy_spanwise_cell,
    eddy_signs,
    eddy_strengths,
    filter_matrices,
    shock_switch,
    dilatation_bin,
    vorticity_bin,
):
    cells_x, span, cells_y = density.shape
    slab_index = lax.axis_index("gx")
    block_index = lax.axis_index("gy")
    slab_count = lax.axis_size("gx")
    fields = jnp.concatenate([density[None], momentum, energy[None]], axis=0)
    total_y = cells_y * lax.axis_size("gy")
    total_eddies = eddy_normal_cell.shape[0] * slab_count
    amplitude = math.sqrt(total_y * span / (total_eddies * SIGMA_Y * SIGMA_Z))
    eddy_weight = (2 * eddy_signs - 1).astype(jnp.float32) * eddy_strengths[:, None] * amplitude
    coords_y = (block_index * cells_y + jnp.arange(cells_y, dtype=jnp.int32)).astype(jnp.float32)
    coords_z = jnp.arange(span, dtype=jnp.int32).astype(jnp.float32)
    partial_sum = inflow_from(
        eddy_normal_cell.astype(jnp.float32),
        eddy_spanwise_cell.astype(jnp.float32),
        eddy_weight,
        coords_y,
        coords_z,
        span,
    )
    inflow = lax.psum(partial_sum, "gx")
    ghost_cells = ghost_state(inflow)
    padded = extended(fields, (("gx", 1), ("gy", 3)), 1)
    padded = padded.at[:, 0, :, 1:-1].set(
        jnp.where(slab_index == 0, ghost_cells, padded[:, 0, :, 1:-1])
    )
    padded = padded.at[:, -1, :, 1:-1].set(
        jnp.where(slab_index == slab_count - 1, fields[:, -1], padded[:, -1, :, 1:-1])
    )
    padded = padded.at[:, 1:-1, :, 0].set(
        jnp.where(block_index == 0, fields[:, :, :, 0], padded[:, 1:-1, :, 0])
    )
    padded = padded.at[:, 1:-1, :, -1].set(
        jnp.where(
            block_index == lax.axis_size("gy") - 1, fields[:, :, :, -1], padded[:, 1:-1, :, -1]
        )
    )
    updated, shock_sensor = section_rhs(padded)
    block_len = filter_matrices.shape[1]
    filter_row = slab_index * cells_x // block_len
    mask_row = lax.dynamic_slice_in_dim(shock_switch, filter_row, 1, 0).astype(jnp.float32)
    weight = mask_row[None] * shock_sensor
    columns = span * cells_y
    stacked = updated.reshape(5, cells_x, columns)
    weight_flat = weight.reshape(1, cells_x, columns)
    pencil, pencil_weight = (
        lax.all_to_all(stacked, "gx", split_axis=2, concat_axis=1, tiled=True),
        lax.all_to_all(weight_flat, "gx", split_axis=2, concat_axis=1, tiled=True),
    )
    smooth = filter_lines(pencil, filter_matrices)
    returned = pencil + pencil_weight * (smooth - pencil)
    back_lines = lax.all_to_all(returned, "gx", split_axis=1, concat_axis=2, tiled=True)
    conserved_next = back_lines.reshape(5, cells_x, span, cells_y)
    partial_histogram = plane_histogram(shock_sensor, dilatation_bin, vorticity_bin)
    summed = lax.psum(partial_histogram, ("gx", "gy"))
    all_cells = cells_x * slab_count * span * total_y
    histogram = summed * (HISTOGRAM_BINS * HISTOGRAM_BINS / all_cells)
    return (conserved_next, histogram)


def solution(mesh):
    in_specs = (
        P("gx", None, "gy"),
        P(None, "gx", None, "gy"),
        P("gx", None, "gy"),
        P("gx"),
        P("gx"),
        P("gx", None),
        P("gx"),
        P(),
        P(None, "gy"),
        P("gx", None, "gy"),
        P("gx", None, "gy"),
    )
    out_specs = (P(None, "gx", None, "gy"), P())
    return jax.shard_map(shards, mesh=mesh, in_specs=in_specs, out_specs=out_specs, check_vma=False)
```

profile of v0, /device:TPU:0, one launch (start us, length us, event | category | flops | bytes accessed | tf_op | source)
XLA Modules:
  0.0 215.9 jit_solution(9551707045615207745)
XLA Ops:
  1.6 1.3 collective-permute-start.1
  2.9 5.5 %collective-permute-start = (f32[5,1,32,32]{3,2,0,1:T(8,128)S(1)}, f32[5,1,32,32]{3,2,0,1:T(8,128)S(1)}, u32[]{:S(2)}, u32[]{:S(2)}) collective-permute-start(f32[5,1,32,32]{3,2,0,1:T(8,128)S(1)} %get-tuple-element.222), channel_id=1, source_target_pairs={{0,2},{2,4},{4,6},{6,8},{8,10},{10,12},{12,14},{14,16},{16,18},{18... | collective-permute-start | bytes 61448 | tf_op jit(solution)/shard_map/ppermute | solution.py:23
  10.8 75.6 %psum.14 = f32[3,32,32]{2,1,0:T(8,128)S(1)} all-reduce(f32[3,32,32]{2,1,0:T(8,128)S(1)} %fusion.50), channel_id=1, replica_groups=mesh['gx'=16,'gy'=2] {'gx'}, use_global_device_ids=true, to_apply=%region_1.2 | all-reduce | flops 3072 | bytes 24576 | tf_op jit(solution)/shard_map/psum | solution.py:153
  91.2 1.3 collective-permute-start.3
  92.5 3.0 %collective-permute-start.2 = (f32[5,10,32,1]{2,3,1,0:T(1,128)S(1)}, f32[5,10,32,1]{2,3,1,0:T(1,128)S(1)}, u32[]{:S(2)}, u32[]{:S(2)}) collective-permute-start(f32[5,10,32,1]{2,3,1,0:T(1,128)S(1)} %copy.81), channel_id=1, source_target_pairs={{0,1},{2,3},{4,5},{6,7},{8,9},{10,11},{12,13},{14,15},{16,17},{18,... | collective-permute-start | bytes 19208 | tf_op jit(solution)/shard_map/ppermute | solution.py:23
  95.5 1.4 and_reduce_fusion
  97.3 1.3 copy.84
  98.6 1.6 pad_maximum_fusion.1
  100.2 1.4 fusion.48
  101.6 1.7 scatter.14
  105.9 3.7 %scatter.19 = f32[5,10,32,34]{3,2,0,1:T(8,128)S(1)} dynamic-update-slice(f32[5,10,32,34]{3,2,0,1:T(8,128)S(1)} %scatter.16, f32[5,8,32,1]{3,2,0,1:T(8,128)S(1)} %slice_select_fusion, s32[]{:T(128)} %constant.328.clone.1, s32[]{:T(128)} %constant.350.clone.1, s32[]{:T(128)} %constant.328.clone.1, s32[]{:T(128)} %constant.351.clone.1) | dynamic-update-slice | bytes 10244 | tf_op jit(solution)/shard_map/scatter | solution.py:165
  114.4 3.7 %reduce.27 = f32[1024,8]{1,0:T(8,128)} reduce(f32[1024,1,8]{2,1,0:T(1,128)} %bitcast.128, f32[]{:T(128)} %broadcast.273), dimensions={1}, to_apply=%bitcast.110.reduce_sub_computation | reduce | bytes 65540
  118.1 1.9 reshape.467
  120.0 3.5 %all-to-all-start.1 = ((f32[16,1,512]{2,1,0:T(1,128)}), f32[16,1,512]{2,1,0:T(1,128)S(1)}, u32[]{:S(2)}, u32[]{:S(2)}) async-start(f32[16,1,512]{2,1,0:T(1,128)} %reshape.467), calls=%async_computation.1 | async-start | bytes 65536 | tf_op jit(solution)/shard_map/all_to_all | solution.py:180
  123.5 2.7 %fusion.14 = f32[5,8,32,32]{3,2,0,1:T(8,128)} fusion(f32[5,10,32,34]{3,2,0,1:T(8,128)S(1)} %get-tuple-element.221, f32[5,10,32,34]{3,2,0,1:T(8,128)S(1)} %scatter.19, f32[5,8,1,32]{3,2,0,1:T(1,128)S(1)} %get-tuple-element.213, f32[5,8,31,32]{3,2,0,1:T(8,128)} %get-tuple-element.215, f32[5,8,31,32]{3,2,0,1:T(8,128)S(1)} %get-tuple-element.214, ...), kind=kLoop, calls=%fused_computation.23 | loop fusion | flops 368640 | bytes 4295680 | tf_op jit(solution)/shard_map/sub | solution.py:75
  126.2 3.6 %copy.122 = f32[5,8,32,32]{1,0,3,2:T(8,128)} copy(f32[5,8,32,32]{3,2,0,1:T(8,128)} %fusion.14) | data formatting | bytes 327680 | tf_op jit(solution)/shard_map/reshape | solution.py:176
  129.8 3.4 %reshape.465 = f32[16,1,2560]{2,1,0:T(1,128)} reshape(f32[1024,5,8]{2,1,0:T(8,128)} %bitcast.117) | data formatting | bytes 327680
  133.1 6.9 %all-to-all-start = ((f32[16,1,2560]{2,1,0:T(1,128)}), f32[16,1,2560]{2,1,0:T(1,128)S(1)}, u32[]{:S(2)}, u32[]{:S(2)}) async-start(f32[16,1,2560]{2,1,0:T(1,128)} %reshape.465), calls=%async_computation | async-start | bytes 327680 | tf_op jit(solution)/shard_map/all_to_all | solution.py:179
  141.8 6.1 %all-to-all-done = f32[16,1,2560]{2,1,0:T(1,128)S(1)} async-done(((f32[16,1,2560]{2,1,0:T(1,128)}), f32[16,1,2560]{2,1,0:T(1,128)S(1)}, u32[]{:S(2)}, u32[]{:S(2)}) %all-to-all-start) | async-done | bytes 163872 | tf_op jit(solution)/shard_map/all_to_all | solution.py:179
  148.9 2.6 %reshape.466 = f32[1024,5,8]{2,1,0:T(8,128)} reshape(f32[16,2560]{1,0:T(8,128)S(1)} %reduce.26) | data formatting | bytes 327680
  151.5 2.6 %copy.103 = f32[5,16,8,64]{3,2,1,0:T(8,128)S(1)} copy(f32[5,16,8,64]{2,0,3,1:T(8,128)} %bitcast.118) | data formatting | bytes 327680 | tf_op jit(solution)/shard_map/all_to_all | solution.py:179
  156.1 3.5 %all-to-all-start.2 = ((f32[16,1,2560]{2,1,0:T(1,128)}), f32[16,1,2560]{2,1,0:T(1,128)S(1)}, u32[]{:S(2)}, u32[]{:S(2)}) async-start(f32[16,1,2560]{2,1,0:T(1,128)} %reshape.469), calls=%async_computation.2 | async-start | bytes 327680 | tf_op jit(solution)/shard_map/all_to_all | solution.py:184
  159.6 12.6 %while.22 = (s32[]{:T(128)}, f32[64,64]{1,0:T(8,128)S(1)}, s32[8,32,32]{2,1,0:T(8,128)}, s32[8,32,32]{2,1,0:T(8,128)}, f32[8,32,32]{2,1,0:T(8,128)S(1)}, /*index=5*/s32[]{:T(128)}, s32[]{:T(128)}) while((s32[]{:T(128)}, f32[64,64]{1,0:T(8,128)S(1)}, s32[8,32,32]{2,1,0:T(8,128)}, s32[8,32,32]{2,1,0:T(8,128)}, ...), condition=%wide.region_4.5_spmd.clone.clone, body=%wide.region_3.4_spmd.clone.clone.sunk | while | flops 50536448 | bytes 94311 | solution.py:113
  172.2 40.8 %psum.15 = f32[64,64]{1,0:T(8,128)S(1)} all-reduce(f32[64,64]{1,0:T(8,128)S(1)} %get-tuple-element.157), channel_id=1, replica_groups=mesh['gx'=16,'gy'=2] {'gx','gy'}, use_global_device_ids=true, to_apply=%region_5.6 | all-reduce | flops 4096 | bytes 32768 | tf_op jit(solution)/shard_map/psum | solution.py:187
  (125 shorter events, 35.6 us)
Async XLA Ops:
  0.6 153.6 %copy-start = (f32[1,128,128]{2,1,0:T(8,128)S(1)}, f32[1,128,128]{2,1,0:T(8,128)}, u32[]{:S(2)}) copy-start(f32[1,128,128]{2,1,0:T(8,128)} %param.40) | copy-start | bytes 196612
  1.6 93.9 %copy-start.4 = (s32[4]{0:T(128)S(1)}, s32[4]{0:T(128)}, u32[]{:S(2)}) copy-start(s32[4]{0:T(128)} %constant.330.clone.1) | copy-start | bytes 52
  1.6 87.3 %collective-permute-start.1 = (f32[5,1,32,32]{3,2,0,1:T(8,128)S(1)}, f32[5,1,32,32]{3,2,0,1:T(8,128)S(1)}, u32[]{:S(2)}, u32[]{:S(2)}) collective-permute-start(f32[5,1,32,32]{3,2,0,1:T(8,128)S(1)} %get-tuple-element.223), channel_id=1, source_target_pairs={{2,0},{4,2},{6,4},{8,6},{10,8},{12,10},{14,12},{16,14},{18,16},{20... | collective-permute-start | bytes 61448 | tf_op jit(solution)/shard_map/ppermute | solution.py:24
  2.9 86.0 %collective-permute-start = (f32[5,1,32,32]{3,2,0,1:T(8,128)S(1)}, f32[5,1,32,32]{3,2,0,1:T(8,128)S(1)}, u32[]{:S(2)}, u32[]{:S(2)}) collective-permute-start(f32[5,1,32,32]{3,2,0,1:T(8,128)S(1)} %get-tuple-element.222), channel_id=1, source_target_pairs={{0,2},{2,4},{4,6},{6,8},{8,10},{10,12},{12,14},{14,16},{16,18},{18... | collective-permute-start | bytes 61448 | tf_op jit(solution)/shard_map/ppermute | solution.py:23
  87.6 11.0 %copy-start.1 = (f32[3,8,32,32]{3,2,1,0:T(8,128)S(1)}, f32[3,8,32,32]{3,2,1,0:T(8,128)}, u32[]{:S(2)}) copy-start(f32[3,8,32,32]{3,2,1,0:T(8,128)} %param.34) | copy-start | bytes 294916
  87.6 11.0 %copy-start.2 = (f32[8,32,32]{2,1,0:T(8,128)S(1)}, f32[8,32,32]{2,1,0:T(8,128)}, u32[]{:S(2)}) copy-start(f32[8,32,32]{2,1,0:T(8,128)} %param.35) | copy-start | bytes 98308
  87.6 11.0 %copy-start.3 = (f32[8,32,32]{2,1,0:T(8,128)S(1)}, f32[8,32,32]{2,1,0:T(8,128)}, u32[]{:S(2)}) copy-start(f32[8,32,32]{2,1,0:T(8,128)} %param.33) | copy-start | bytes 98308
  91.2 6.1 %collective-permute-start.3 = (f32[5,10,32,1]{2,3,1,0:T(1,128)S(1)}, f32[5,10,32,1]{2,3,1,0:T(1,128)S(1)}, u32[]{:S(2)}, u32[]{:S(2)}) collective-permute-start(f32[5,10,32,1]{2,3,1,0:T(1,128)S(1)} %copy.82), channel_id=1, source_target_pairs={{1,0},{3,2},{5,4},{7,6},{9,8},{11,10},{13,12},{15,14},{17,16},{19,... | collective-permute-start | bytes 19208 | tf_op jit(solution)/shard_map/ppermute | solution.py:24
  92.5 4.4 %collective-permute-start.2 = (f32[5,10,32,1]{2,3,1,0:T(1,128)S(1)}, f32[5,10,32,1]{2,3,1,0:T(1,128)S(1)}, u32[]{:S(2)}, u32[]{:S(2)}) collective-permute-start(f32[5,10,32,1]{2,3,1,0:T(1,128)S(1)} %copy.81), channel_id=1, source_target_pairs={{0,1},{2,3},{4,5},{6,7},{8,9},{10,11},{12,13},{14,15},{16,17},{18,... | collective-permute-start | bytes 19208 | tf_op jit(solution)/shard_map/ppermute | solution.py:23
  120.0 13.2 %all-to-all-start.1 = ((f32[16,1,512]{2,1,0:T(1,128)}), f32[16,1,512]{2,1,0:T(1,128)S(1)}, u32[]{:S(2)}, u32[]{:S(2)}) async-start(f32[16,1,512]{2,1,0:T(1,128)} %reshape.467), calls=%async_computation.1 | async-start | bytes 65536 | tf_op jit(solution)/shard_map/all_to_all | solution.py:180
  133.1 14.8 %all-to-all-start = ((f32[16,1,2560]{2,1,0:T(1,128)}), f32[16,1,2560]{2,1,0:T(1,128)S(1)}, u32[]{:S(2)}, u32[]{:S(2)}) async-start(f32[16,1,2560]{2,1,0:T(1,128)} %reshape.465), calls=%async_computation | async-start | bytes 327680 | tf_op jit(solution)/shard_map/all_to_all | solution.py:179
  156.1 57.5 %all-to-all-start.2 = ((f32[16,1,2560]{2,1,0:T(1,128)}), f32[16,1,2560]{2,1,0:T(1,128)S(1)}, u32[]{:S(2)}, u32[]{:S(2)}) async-start(f32[16,1,2560]{2,1,0:T(1,128)} %reshape.469), calls=%async_computation.2 | async-start | bytes 327680 | tf_op jit(solution)/shard_map/all_to_all | solution.py:184
where the time goes:
time: 218 us; the launch traced here: 216 us
  blocking collectives  116 us (53%)
  local copies, waits for them, and re-layouts  39.7 us (18%)
  starting transfers between devices  25 us (11%)
  other arithmetic  21.8 us (10%)
  waiting for transfers between devices  6.13 us (3%)
  matrix products  5.55 us (3%)
    psum x1, blocking collectives, shards(): inflow = lax.psum(partial_sum, 'gx')  75.6 us
    psum x1, blocking collectives, shards(): summed = lax.psum(partial_histogram, ('gx', 'gy'))  40.8 us
    unnamed x16, local copies, waits for them, and re-layouts  9.82 us
    ppermute x2, starting transfers between devices, extended(): before = lax.ppermute(last, axis, up)  8.5 us
    all_to_all x1, starting transfers between devices, shards(): lax.all_to_all(stacked, 'gx', split_axis=2, concat_axis=1, tiled=True)  6.88 us
    all_to_all x1, waiting for transfers between devices, shards(): lax.all_to_all(stacked, 'gx', split_axis=2, concat_axis=1, tiled=True)  6.11 us
    dynamic_slice x16, local copies, waits for them, and re-layouts, plane_histogram(): lax.scan(accumulate_plane, jnp.zeros((HISTOGRAM_BINS, HISTOGRAM_BINS), jn...  6 us
    dot_general x8, matrix products, accumulate_plane(): jnp.dot(dilatation_table, vorticity_table, precision=lax.Precision.HIGHEST)  4.61 us
  transfers between devices with their start and end apart: 7, of which 1 were waited for; matrix products, arithmetic and copies ran while one was open for 14% of the time, Pallas kernels for 0%

commit v1 on v0

--- a/solution.py
+++ b/solution.py
@@ -184,7 +184,7 @@
     back_lines = lax.all_to_all(returned, "gx", split_axis=1, concat_axis=2, tiled=True)
     conserved_next = back_lines.reshape(5, cells_x, span, cells_y)
     partial_histogram = plane_histogram(shock_sensor, dilatation_bin, vorticity_bin)
-    summed = lax.psum(partial_histogram, ("gx", "gy"))
+    summed = lax.psum(lax.psum(partial_histogram, "gy"), "gx")
     all_cells = cells_x * slab_count * span * total_y
     histogram = summed * (HISTOGRAM_BINS * HISTOGRAM_BINS / all_cells)
     return (conserved_next, histogram)

time: 218 us -> 258 us (1.18)
  blocking collectives: 116 us -> 156 us
    psum x1 -> x2, blocking collectives: 40.8 us -> 80.5 us  [shards(): summed = lax.psum(lax.psum(partial_histogram, 'gy'), 'gx')]
  transfers between devices with their start and end apart: 7 -> 7, of which waited for: 1 -> 1; matrix products, arithmetic and copies ran while one was open for 14% -> 12% of each run, Pallas kernels for 0% -> 0%
where the time goes in v1:
time: 258 us; the launch traced here: 256 us
  blocking collectives  156 us (60%)
  local copies, waits for them, and re-layouts  39.8 us (15%)
  starting transfers between devices  25 us (10%)
  other arithmetic  22.1 us (9%)
  waiting for transfers between devices  6.05 us (2%)
  matrix products  5.56 us (2%)
    psum x2, blocking collectives, shards(): summed = lax.psum(lax.psum(partial_histogram, 'gy'), 'gx')  80.5 us
    psum x1, blocking collectives, shards(): inflow = lax.psum(partial_sum, 'gx')  75.6 us
    unnamed x16, local copies, waits for them, and re-layouts  9.81 us
    ppermute x2, starting transfers between devices, extended(): before = lax.ppermute(last, axis, up)  8.5 us
    all_to_all x1, starting transfers between devices, shards(): lax.all_to_all(stacked, 'gx', split_axis=2, concat_axis=1, tiled=True)  6.88 us
    all_to_all x1, waiting for transfers between devices, shards(): lax.all_to_all(stacked, 'gx', split_axis=2, concat_axis=1, tiled=True)  6.04 us
    dynamic_slice x16, local copies, waits for them, and re-layouts, plane_histogram(): lax.scan(accumulate_plane, jnp.zeros((HISTOGRAM_BINS, HISTOGRAM_BINS), jn...  6 us
  transfers between devices with their start and end apart: 7, of which 1 were waited for; matrix products, arithmetic and copies ran while one was open for 12% of the time, Pallas kernels for 0%

profile of v1, /device:TPU:0, one launch (start us, length us, event | category | flops | bytes accessed | tf_op | source)
XLA Modules:
  0.0 256.0 jit_solution(4723747580588940098)
XLA Ops:
  1.6 1.3 collective-permute-start.1
  2.9 5.5 %collective-permute-start = (f32[5,1,32,32]{3,2,0,1:T(8,128)S(1)}, f32[5,1,32,32]{3,2,0,1:T(8,128)S(1)}, u32[]{:S(2)}, u32[]{:S(2)}) collective-permute-start(f32[5,1,32,32]{3,2,0,1:T(8,128)S(1)} %get-tuple-element.222), channel_id=1, source_target_pairs={{0,2},{2,4},{4,6},{6,8},{8,10},{10,12},{12,14},{14,16},{16,18},{18... | collective-permute-start | bytes 61448 | tf_op jit(solution)/shard_map/ppermute | solution.py:23
  10.8 75.6 %psum.21 = f32[3,32,32]{2,1,0:T(8,128)S(1)} all-reduce(f32[3,32,32]{2,1,0:T(8,128)S(1)} %fusion.50), channel_id=1, replica_groups=mesh['gx'=16,'gy'=2] {'gx'}, use_global_device_ids=true, to_apply=%region_1.2 | all-reduce | flops 3072 | bytes 24576 | tf_op jit(solution)/shard_map/psum | solution.py:153
  91.2 1.3 collective-permute-start.3
  92.5 3.0 %collective-permute-start.2 = (f32[5,10,32,1]{2,3,1,0:T(1,128)S(1)}, f32[5,10,32,1]{2,3,1,0:T(1,128)S(1)}, u32[]{:S(2)}, u32[]{:S(2)}) collective-permute-start(f32[5,10,32,1]{2,3,1,0:T(1,128)S(1)} %copy.81), channel_id=1, source_target_pairs={{0,1},{2,3},{4,5},{6,7},{8,9},{10,11},{12,13},{14,15},{16,17},{18,... | collective-permute-start | bytes 19208 | tf_op jit(solution)/shard_map/ppermute | solution.py:23
  95.5 1.4 and_reduce_fusion
  98.6 1.6 pad_maximum_fusion.1
  100.2 1.4 fusion.48
  101.6 1.7 scatter.14
  105.9 3.7 %scatter.19 = f32[5,10,32,34]{3,2,0,1:T(8,128)S(1)} dynamic-update-slice(f32[5,10,32,34]{3,2,0,1:T(8,128)S(1)} %scatter.16, f32[5,8,32,1]{3,2,0,1:T(8,128)S(1)} %slice_select_fusion, s32[]{:T(128)} %constant.328.clone.1, s32[]{:T(128)} %constant.350.clone.1, s32[]{:T(128)} %constant.328.clone.1, s32[]{:T(128)} %constant.351.clone.1) | dynamic-update-slice | bytes 10244 | tf_op jit(solution)/shard_map/scatter | solution.py:165
  114.4 3.8 %reduce.27 = f32[1024,8]{1,0:T(8,128)} reduce(f32[1024,1,8]{2,1,0:T(1,128)} %bitcast.128, f32[]{:T(128)} %broadcast.273), dimensions={1}, to_apply=%bitcast.110.reduce_sub_computation | reduce | bytes 65540
  118.2 1.9 reshape.467
  120.1 3.5 %all-to-all-start.1 = ((f32[16,1,512]{2,1,0:T(1,128)}), f32[16,1,512]{2,1,0:T(1,128)S(1)}, u32[]{:S(2)}, u32[]{:S(2)}) async-start(f32[16,1,512]{2,1,0:T(1,128)} %reshape.467), calls=%async_computation.1 | async-start | bytes 65536 | tf_op jit(solution)/shard_map/all_to_all | solution.py:180
  123.6 2.7 %fusion.14 = f32[5,8,32,32]{3,2,0,1:T(8,128)} fusion(f32[5,10,32,34]{3,2,0,1:T(8,128)S(1)} %get-tuple-element.221, f32[5,10,32,34]{3,2,0,1:T(8,128)S(1)} %scatter.19, f32[5,8,1,32]{3,2,0,1:T(1,128)S(1)} %get-tuple-element.213, f32[5,8,31,32]{3,2,0,1:T(8,128)} %get-tuple-element.215, f32[5,8,31,32]{3,2,0,1:T(8,128)S(1)} %get-tuple-element.214, ...), kind=kLoop, calls=%fused_computation.23 | loop fusion | flops 368640 | bytes 4295680 | tf_op jit(solution)/shard_map/sub | solution.py:75
  126.3 3.6 %copy.122 = f32[5,8,32,32]{1,0,3,2:T(8,128)} copy(f32[5,8,32,32]{3,2,0,1:T(8,128)} %fusion.14) | data formatting | bytes 327680 | tf_op jit(solution)/shard_map/reshape | solution.py:176
  129.9 3.4 %reshape.465 = f32[16,1,2560]{2,1,0:T(1,128)} reshape(f32[1024,5,8]{2,1,0:T(8,128)} %bitcast.117) | data formatting | bytes 327680
  133.3 6.9 %all-to-all-start = ((f32[16,1,2560]{2,1,0:T(1,128)}), f32[16,1,2560]{2,1,0:T(1,128)S(1)}, u32[]{:S(2)}, u32[]{:S(2)}) async-start(f32[16,1,2560]{2,1,0:T(1,128)} %reshape.465), calls=%async_computation | async-start | bytes 327680 | tf_op jit(solution)/shard_map/all_to_all | solution.py:179
  142.1 6.0 %all-to-all-done = f32[16,1,2560]{2,1,0:T(1,128)S(1)} async-done(((f32[16,1,2560]{2,1,0:T(1,128)}), f32[16,1,2560]{2,1,0:T(1,128)S(1)}, u32[]{:S(2)}, u32[]{:S(2)}) %all-to-all-start) | async-done | bytes 163872 | tf_op jit(solution)/shard_map/all_to_all | solution.py:179
  149.1 2.6 %reshape.466 = f32[1024,5,8]{2,1,0:T(8,128)} reshape(f32[16,2560]{1,0:T(8,128)S(1)} %reduce.26) | data formatting | bytes 327680
  151.7 2.6 %copy.103 = f32[5,16,8,64]{3,2,1,0:T(8,128)S(1)} copy(f32[5,16,8,64]{2,0,3,1:T(8,128)} %bitcast.118) | data formatting | bytes 327680 | tf_op jit(solution)/shard_map/all_to_all | solution.py:179
  156.3 3.5 %all-to-all-start.2 = ((f32[16,1,2560]{2,1,0:T(1,128)}), f32[16,1,2560]{2,1,0:T(1,128)S(1)}, u32[]{:S(2)}, u32[]{:S(2)}) async-start(f32[16,1,2560]{2,1,0:T(1,128)} %reshape.469), calls=%async_computation.2 | async-start | bytes 327680 | tf_op jit(solution)/shard_map/all_to_all | solution.py:184
  159.8 12.6 %while.22 = (s32[]{:T(128)}, f32[64,64]{1,0:T(8,128)S(1)}, s32[8,32,32]{2,1,0:T(8,128)}, s32[8,32,32]{2,1,0:T(8,128)}, f32[8,32,32]{2,1,0:T(8,128)S(1)}, /*index=5*/s32[]{:T(128)}, s32[]{:T(128)}) while((s32[]{:T(128)}, f32[64,64]{1,0:T(8,128)S(1)}, s32[8,32,32]{2,1,0:T(8,128)}, s32[8,32,32]{2,1,0:T(8,128)}, ...), condition=%wide.region_4.5_spmd.clone.clone, body=%wide.region_3.4_spmd.clone.clone.sunk | while | flops 50536448 | bytes 94311 | solution.py:113
  172.4 3.4 %psum.22 = f32[64,64]{1,0:T(8,128)S(1)} all-reduce(f32[64,64]{1,0:T(8,128)S(1)} %get-tuple-element.157), channel_id=1, replica_groups=mesh['gx'=16,'gy'=2] {'gy'}, use_global_device_ids=true, to_apply=%region_5.6 | all-reduce | flops 4096 | bytes 32768 | tf_op jit(solution)/shard_map/psum | solution.py:187
  175.8 77.1 %psum.23 = f32[64,64]{1,0:T(8,128)S(1)} all-reduce(f32[64,64]{1,0:T(8,128)S(1)} %psum.22), channel_id=1, replica_groups=mesh['gx'=16,'gy'=2] {'gx'}, use_global_device_ids=true, to_apply=%region_6.7 | all-reduce | flops 4096 | bytes 32768 | tf_op jit(solution)/shard_map/psum | solution.py:187
  (126 shorter events, 37.1 us)
Async XLA Ops:
  0.6 153.8 %copy-start = (f32[1,128,128]{2,1,0:T(8,128)S(1)}, f32[1,128,128]{2,1,0:T(8,128)}, u32[]{:S(2)}) copy-start(f32[1,128,128]{2,1,0:T(8,128)} %param.40) | copy-start | bytes 196612
  1.6 93.9 %copy-start.4 = (s32[4]{0:T(128)S(1)}, s32[4]{0:T(128)}, u32[]{:S(2)}) copy-start(s32[4]{0:T(128)} %constant.330.clone.1) | copy-start | bytes 52
  1.6 87.3 %collective-permute-start.1 = (f32[5,1,32,32]{3,2,0,1:T(8,128)S(1)}, f32[5,1,32,32]{3,2,0,1:T(8,128)S(1)}, u32[]{:S(2)}, u32[]{:S(2)}) collective-permute-start(f32[5,1,32,32]{3,2,0,1:T(8,128)S(1)} %get-tuple-element.223), channel_id=1, source_target_pairs={{2,0},{4,2},{6,4},{8,6},{10,8},{12,10},{14,12},{16,14},{18,16},{20... | collective-permute-start | bytes 61448 | tf_op jit(solution)/shard_map/ppermute | solution.py:24
  2.9 86.0 %collective-permute-start = (f32[5,1,32,32]{3,2,0,1:T(8,128)S(1)}, f32[5,1,32,32]{3,2,0,1:T(8,128)S(1)}, u32[]{:S(2)}, u32[]{:S(2)}) collective-permute-start(f32[5,1,32,32]{3,2,0,1:T(8,128)S(1)} %get-tuple-element.222), channel_id=1, source_target_pairs={{0,2},{2,4},{4,6},{6,8},{8,10},{10,12},{12,14},{14,16},{16,18},{18... | collective-permute-start | bytes 61448 | tf_op jit(solution)/shard_map/ppermute | solution.py:23
  87.6 11.0 %copy-start.1 = (f32[3,8,32,32]{3,2,1,0:T(8,128)S(1)}, f32[3,8,32,32]{3,2,1,0:T(8,128)}, u32[]{:S(2)}) copy-start(f32[3,8,32,32]{3,2,1,0:T(8,128)} %param.34) | copy-start | bytes 294916
  87.6 11.0 %copy-start.2 = (f32[8,32,32]{2,1,0:T(8,128)S(1)}, f32[8,32,32]{2,1,0:T(8,128)}, u32[]{:S(2)}) copy-start(f32[8,32,32]{2,1,0:T(8,128)} %param.35) | copy-start | bytes 98308
  87.6 11.0 %copy-start.3 = (f32[8,32,32]{2,1,0:T(8,128)S(1)}, f32[8,32,32]{2,1,0:T(8,128)}, u32[]{:S(2)}) copy-start(f32[8,32,32]{2,1,0:T(8,128)} %param.33) | copy-start | bytes 98308
  91.2 6.1 %collective-permute-start.3 = (f32[5,10,32,1]{2,3,1,0:T(1,128)S(1)}, f32[5,10,32,1]{2,3,1,0:T(1,128)S(1)}, u32[]{:S(2)}, u32[]{:S(2)}) collective-permute-start(f32[5,10,32,1]{2,3,1,0:T(1,128)S(1)} %copy.82), channel_id=1, source_target_pairs={{1,0},{3,2},{5,4},{7,6},{9,8},{11,10},{13,12},{15,14},{17,16},{19,... | collective-permute-start | bytes 19208 | tf_op jit(solution)/shard_map/ppermute | solution.py:24
  92.5 4.4 %collective-permute-start.2 = (f32[5,10,32,1]{2,3,1,0:T(1,128)S(1)}, f32[5,10,32,1]{2,3,1,0:T(1,128)S(1)}, u32[]{:S(2)}, u32[]{:S(2)}) collective-permute-start(f32[5,10,32,1]{2,3,1,0:T(1,128)S(1)} %copy.81), channel_id=1, source_target_pairs={{0,1},{2,3},{4,5},{6,7},{8,9},{10,11},{12,13},{14,15},{16,17},{18,... | collective-permute-start | bytes 19208 | tf_op jit(solution)/shard_map/ppermute | solution.py:23
  120.1 13.2 %all-to-all-start.1 = ((f32[16,1,512]{2,1,0:T(1,128)}), f32[16,1,512]{2,1,0:T(1,128)S(1)}, u32[]{:S(2)}, u32[]{:S(2)}) async-start(f32[16,1,512]{2,1,0:T(1,128)} %reshape.467), calls=%async_computation.1 | async-start | bytes 65536 | tf_op jit(solution)/shard_map/all_to_all | solution.py:180
  133.3 14.8 %all-to-all-start = ((f32[16,1,2560]{2,1,0:T(1,128)}), f32[16,1,2560]{2,1,0:T(1,128)S(1)}, u32[]{:S(2)}, u32[]{:S(2)}) async-start(f32[16,1,2560]{2,1,0:T(1,128)} %reshape.465), calls=%async_computation | async-start | bytes 327680 | tf_op jit(solution)/shard_map/all_to_all | solution.py:179
  156.3 97.3 %all-to-all-start.2 = ((f32[16,1,2560]{2,1,0:T(1,128)}), f32[16,1,2560]{2,1,0:T(1,128)S(1)}, u32[]{:S(2)}, u32[]{:S(2)}) async-start(f32[16,1,2560]{2,1,0:T(1,128)} %reshape.469), calls=%async_computation.2 | async-start | bytes 327680 | tf_op jit(solution)/shard_map/all_to_all | solution.py:184
